TPU v7x, 32 devices: a whole 2x2x4 slice. The times are simulated.
32 devices in a mesh: guide: 2 (over core), blk: 16 (over z, y, x).
Axes of the slice: x: 2, y: 2, z: 4, core: 2. Of those that a mesh axis runs over, the one named last changes fastest.
Arguments:
- x_cols: bfloat16 [128, 2048], P(None, 'blk'), may hold values from -3 to 3
- queries: bfloat16 [128, 9216], P('blk'), may hold values from -64 to 64
- new_kv: bfloat16 [128, 576], P('blk'), may hold values from -6 to 6
- cache: bfloat16 [2, 128, 256, 576], P('guide', 'blk'), may hold values from -8 to 8
- lengths: int32 [2, 128], P('guide'), may hold values from 2 to 256, as said below
- perm: int32 [128], replicated, may hold values from 0 to 127, each once
- guide_scale: float32 [128], replicated, may hold values from 1.5 to 7.5
- w_uv: bfloat16 [16, 512, 128], replicated, may hold values from -0.75 to 0.75
- w_out: bfloat16 [2048, 2048], P(None, 'blk'), may hold values from -0.125 to 0.125
- mlp_gain: float32 [2048], replicated, may hold values from 0.5 to 1.5
- w_gate: bfloat16 [2048, 10944], P(None, 'blk'), may hold values from -0.125 to 0.125
- w_up: bfloat16 [2048, 10944], P(None, 'blk'), may hold values from -0.125 to 0.125
- w_down: bfloat16 [10944, 2048], P('blk'), may hold values from -0.0546875 to 0.0546875
- head_gain: float32 [2048], replicated, may hold values from 0.5 to 1.5
- w_head: bfloat16 [2048, 102400], P(None, 'blk'), may hold values from -0.125 to 0.125
Outputs:
- guided: bfloat16 [128, 102400], P('guide', 'blk')
Inputs may be any that keep to these rules, and one draw needn't show every extreme that they name: Positions 0 to lengths[g, r] - 1 of request r's cache in group g are live; each group has a request with 256 live positions. Slot s holds request perm[s]; every request has one slot.
All inputs are finite; a program needn't handle non-finite values.
Results may differ from a plain program's by a relative error of at most 0.018.
Values may be sent and summed in bfloat16 or wider, within the bound.
No kernel may reach another device: no remote copies, remote signals or barrier semaphores. Data moves between devices by JAX's collectives and lax.ppermute only.
A program may use at most 128 MiB of HBM per device.

v0:
```python
import jax
import jax.numpy as jnp
from jax import lax
from jax.sharding import PartitionSpec as P

FF = 10944


def partner(value, axis, apart):
    mask = 2**apart
    pairs = [(source, source ^ mask) for source in range(lax.axis_size(axis))]
    return lax.ppermute(value, axis, pairs)


def rms_round(hidden, gain):
    values = hidden.astype(jnp.float32)
    meansq = jnp.mean(values * values, axis=-1, keepdims=True)
    return (values * lax.rsqrt(meansq + 1e-06) * gain).astype(jnp.bfloat16)


def body(
    x_cols,
    queries,
    new_kv,
    cache,
    lengths,
    perm,
    guide_scale,
    w_uv,
    w_out,
    mlp_gain,
    w_gate,
    w_up,
    w_down,
    head_gain,
    w_head,
):
    guide_index = lax.axis_index("guide")
    blk_index = lax.axis_index("blk")
    slots_dev = queries.shape[0]
    heads_count = w_uv.shape[0]
    latent_size = w_uv.shape[1]
    key_width = new_kv.shape[1]
    score_scale = (w_uv.shape[2] + key_width - latent_size) ** (-0.5)
    slot_ids = blk_index * slots_dev + jnp.arange(slots_dev, dtype=jnp.int32)
    owners = jnp.take(perm, slot_ids)
    live_len = jnp.take(lengths[0], owners)
    query_heads = queries.reshape(slots_dev, heads_count, key_width)
    cached_keys = cache[0]
    scores = (
        jnp.einsum("shk,slk->shl", query_heads, cached_keys, preferred_element_type=jnp.float32)
        * score_scale
    )
    own_score = (
        jnp.einsum("shk,sk->sh", query_heads, new_kv, preferred_element_type=jnp.float32)
        * score_scale
    )
    live_mask = (
        jnp.arange(cached_keys.shape[1], dtype=jnp.int32)[None, None, :] < live_len[:, None, None]
    )
    scores = jnp.where(live_mask, scores, jnp.float32(-1e30))
    peak_score = jnp.maximum(jnp.max(scores, axis=-1), own_score)
    probs = jnp.where(live_mask, jnp.exp(scores - peak_score[..., None]), jnp.float32(0.0))
    own_prob = jnp.exp(own_score - peak_score)
    softmax_total = jnp.sum(probs, axis=-1) + own_prob
    weights = (probs / softmax_total[..., None]).astype(jnp.bfloat16)
    own_weight = (own_prob / softmax_total).astype(jnp.bfloat16)
    latent_out = jnp.einsum(
        "shl,slc->shc", weights, cached_keys[:, :, :latent_size], preferred_element_type=jnp.float32
    )
    latent_out = latent_out + own_weight.astype(jnp.float32)[..., None] * new_kv[
        :, None, :latent_size
    ].astype(jnp.float32)
    value_rows = jnp.einsum(
        "shc,hcd->shd", latent_out.astype(jnp.bfloat16), w_uv, preferred_element_type=jnp.float32
    )
    value_rows = value_rows.astype(jnp.bfloat16).reshape(slots_dev, -1)
    attended = jnp.dot(
        lax.all_gather(value_rows, "blk", axis=0, tiled=True),
        w_out,
        preferred_element_type=jnp.float32,
    )
    residual = (x_cols.astype(jnp.float32) + attended).astype(jnp.bfloat16)
    rows_full = lax.all_gather(residual, "blk", axis=1, tiled=True)
    normed = rms_round(rows_full, mlp_gain)
    unit_count = w_gate.shape[1]
    gate_out = jnp.dot(normed, w_gate, preferred_element_type=jnp.float32)
    up_out = jnp.dot(normed, w_up, preferred_element_type=jnp.float32)
    unit_ids = blk_index * unit_count + jnp.arange(unit_count, dtype=jnp.int32)
    hidden = jnp.where(
        unit_ids[None, :] < FF, jax.nn.silu(gate_out) * up_out, jnp.float32(0.0)
    ).astype(jnp.bfloat16)
    partial_sum = jnp.dot(hidden, w_down, preferred_element_type=jnp.float32)
    summed = lax.psum(partial_sum, "blk")
    after_mlp = (rows_full.astype(jnp.float32) + summed).astype(jnp.bfloat16)
    logits = jnp.dot(rms_round(after_mlp, head_gain), w_head, preferred_element_type=jnp.float32)
    request_count = logits.shape[0]
    half_rows = request_count // 2
    slot_scale = jnp.take(guide_scale, perm)
    request_order = (
        jnp.zeros((request_count,), jnp.int32)
        .at[perm]
        .set(jnp.arange(request_count, dtype=jnp.int32))
    )
    own_order = lax.dynamic_slice_in_dim(request_order, guide_index * half_rows, half_rows)
    other_logits = partner(logits.astype(jnp.bfloat16), "guide", 0).astype(logits.dtype)
    cond_logits = jnp.where(guide_index == 0, logits, other_logits)
    uncond_logits = jnp.where(guide_index == 0, other_logits, logits)
    mixed = (uncond_logits + slot_scale[:, None] * (cond_logits - uncond_logits)).astype(
        jnp.bfloat16
    )
    return jnp.take(mixed, own_order, axis=0)


def solution(mesh):
    return jax.shard_map(
        body,
        mesh=mesh,
        in_specs=(
            P(None, "blk"),
            P("blk", None),
            P("blk", None),
            P("guide", "blk", None, None),
            P("guide", None),
            P(),
            P(),
            P(),
            P(None, "blk"),
            P(),
            P(None, "blk"),
            P(None, "blk"),
            P("blk", None),
            P(),
            P(None, "blk"),
        ),
        out_specs=P("guide", "blk"),
        check_vma=False,
    )
```

profile of v0, /device:TPU:0, one launch (start us, length us, event | category | flops | bytes accessed | tf_op | source)
XLA Modules:
  0.0 257.7 jit_solution(10083849745343940406)
XLA Ops:
  6.5 0.0 copy-start
  6.5 0.0 all-reduce.2.cloned.1.call-start
  6.5 1.2 reshape.73
  7.8 1.3 gather_fusion.2
  9.1 1.3 gather_fusion.3
  10.4 0.1 iota_compare_fusion
  10.5 0.7 slice_convert_fusion
  11.2 0.9 fusion.44
  12.1 2.2 fusion.55
  14.3 0.2 fusion.39
  14.5 0.1 copy.17
  14.6 0.0 copy-start.3
  14.6 0.0 copy-start.4
  14.6 0.0 copy-start.6
  14.6 2.4 fusion.4
  17.0 0.0 copy-done.3
  17.0 0.0 copy-start.7
  17.0 0.5 fusion.11
  17.5 45.3 %all_gather.6 = bf16[128,2048]{1,0:T(8,128)(2,1)S(1)} all-gather(bf16[8,2048]{1,0:T(8,128)(2,1)S(1)} %fusion.11), channel_id=1, replica_groups=mesh['guide'=2,'blk'=16] {'blk'}, dimensions={0}, use_global_device_ids=true | all-gather | bytes 557056 | tf_op jit(solution)/shard_map/all_gather | solution.py:79
  62.8 0.0 copy-done.4
  62.8 0.0 copy-done.6
  62.8 0.3 fusion.10
  63.1 38.5 %all_gather.7 = bf16[128,2048]{1,0:T(8,128)(2,1)S(1)} all-gather(bf16[128,128]{1,0:T(8,128)(2,1)S(1)} %fusion.10), channel_id=1, replica_groups=mesh['guide'=2,'blk'=16] {'blk'}, dimensions={1}, use_global_device_ids=true | all-gather | bytes 557056 | tf_op jit(solution)/shard_map/all_gather | solution.py:84
  101.7 0.2 fusion.15
  101.9 0.0 copy-done.7
  101.9 3.5 %fusion.34 = f32[128,684]{0,1:T(8,128)} fusion(bf16[2048,684]{0,1:T(8,128)(2,1)} %param.27, bf16[128,2048]{1,0:T(8,128)(2,1)S(1)} %all_gather.7, f32[2048]{0:T(1024)S(1)} %copy-done.7, f32[128]{0:T(128)S(1)} %add_rsqrt_fusion.1), kind=kOutput, calls=%fused_computation.49 | convolution fusion | flops 359661568 | bytes 3684864 | tf_op jit(solution)/shard_map/dot_general | solution.py:87
  105.4 0.0 copy-done
  105.4 0.0 copy-start.5
  105.4 5.0 %fusion.8 = f32[128,2048]{1,0:T(8,128)} fusion(bf16[684,2048]{1,0:T(8,128)(2,1)S(1)} %copy-done, bf16[2048,684]{0,1:T(8,128)(2,1)} %param.28, f32[128,684]{0,1:T(8,128)} %fusion.34, pred[684]{0:T(1024)(128)(4,1)S(1)} %add_compare_fusion, bf16[128,2048]{1,0:T(8,128)(2,1)S(1)} %all_gather.7, f32[2048]{0:T(1024)S(1)} %copy-done.7, f32[128]{0:T(128)S(1)} %add_rsqrt_fusion.1), kind=kOutput, calls=%fused_computation.21 | convolution fusion | flops 718887424 | bytes 7535788 | tf_op jit(solution)/shard_map/dot_general | solution.py:93
  110.4 0.0 all-reduce.2.cloned.1.call-update
  110.5 109.6 %all-reduce.2.cloned.1.call-done = f32[128,2048]{1,0:T(8,128)} async-done(((f32[128,2048]{1,0:T(8,128)}), f32[128,2048]{1,0:T(8,128)}) %all-reduce.2.cloned.1.call-update) | async-done | bytes 1048592 | tf_op jit(solution)/shard_map/psum | solution.py:94
  220.1 1.4 fusion.12
  221.5 0.0 copy-done.5
  221.5 0.0 copy-start.2
  221.5 0.0 copy-start.1
  221.5 14.7 %fusion.56 = (bf16[128,6400]{1,0:T(8,128)(2,1)}, f32[128,6400]{1,0:T(8,128)}) fusion(bf16[2048,6400]{1,0:T(8,128)(2,1)} %param.31, f32[2048]{0:T(1024)S(1)} %copy-done.5, f32[128]{0:T(128)S(1)} %add_rsqrt_fusion, f32[128,2048]{1,0:T(8,128)} %all-reduce.2.cloned.1.call-done, bf16[128,2048]{1,0:T(8,128)(2,1)S(1)} %all_gather.7), kind=kOutput, calls=%fused_computation.90 | convolution fusion | flops 3358097408 | bytes 32711168 | tf_op jit(solution)/shard_map/dot_general | solution.py:96
  236.2 0.0 collective-permute-start
  236.2 0.0 copy-done.2
  236.2 1.2 scatter_custom_fusion
  237.4 0.0 copy-done.1
  237.4 1.2 gather_fusion
  238.6 0.1 compare_and_fusion
  238.8 1.3 collective-permute-done
  240.1 4.3 %fusion.3 = bf16[128,6400]{1,0:T(8,128)(2,1)} fusion(f32[128,6400]{1,0:T(8,128)} %get-tuple-element.13, bf16[128,6400]{1,0:T(8,128)(2,1)} %collective-permute-done, f32[128]{0:T(128)S(1)} %and_select_fusion.2, pred[]{:T(512)S(6)} %eq.4), kind=kLoop, calls=%fused_computation.10 | loop fusion | flops 5734400 | bytes 6554113 | tf_op jit(solution)/shard_map/convert_element_type | solution.py:109
  244.4 4.3 %gather_fusion.1 = bf16[64,6400]{1,0:T(8,128)(2,1)} fusion(bf16[128,6400]{1,0:T(8,128)(2,1)} %fusion.3, s32[1024]{0:T(1024)S(1)} %pad_clamp_fusion), kind=kCustom, calls=%fused_computation.3 | custom fusion | bytes 1638656 | tf_op jit(solution)/shard_map/jit(_take)/gather | solution.py:112
  248.7 2.2 broadcast_select_fusion
  (15 shorter events, 0.1 us)
Async XLA Ops:
  6.5 98.9 %copy-start = (bf16[684,2048]{1,0:T(8,128)(2,1)S(1)}, bf16[684,2048]{1,0:T(8,128)(2,1)}, u32[]{:S(2)}) copy-start(bf16[684,2048]{1,0:T(8,128)(2,1)} %param.29) | copy-start | bytes 8404996
  6.5 213.5 %all-reduce.2.cloned.1.call-start = ((), (), s32[]{:S(2)}) async-start(), calls=%async_computation | async-start | bytes 2097152 | tf_op jit(solution)/shard_map/psum | solution.py:94
  14.6 2.4 copy-start.3
  14.6 48.3 %copy-start.4 = (bf16[2048,128]{1,0:T(8,128)(2,1)S(1)}, bf16[2048,128]{1,0:T(8,128)(2,1)}, u32[]{:S(2)}) copy-start(bf16[2048,128]{1,0:T(8,128)(2,1)} %param.25) | copy-start | bytes 1572868
  14.6 48.3 %copy-start.6 = (bf16[128,128]{1,0:T(8,128)(2,1)S(1)}, bf16[128,128]{1,0:T(8,128)(2,1)}, u32[]{:S(2)}) copy-start(bf16[128,128]{1,0:T(8,128)(2,1)} %param.17) | copy-start | bytes 98308
  17.0 84.9 %copy-start.7 = (f32[2048]{0:T(1024)S(1)}, f32[2048]{0:T(1024)}, u32[]{:S(2)}) copy-start(f32[2048]{0:T(1024)} %param.26) | copy-start | bytes 24580
  105.4 116.1 %copy-start.5 = (f32[2048]{0:T(1024)S(1)}, f32[2048]{0:T(1024)}, u32[]{:S(2)}) copy-start(f32[2048]{0:T(1024)} %param.30) | copy-start | bytes 24580
  221.5 14.7 %copy-start.2 = (s32[128]{0:T(128)S(1)}, s32[128]{0:T(128)}, u32[]{:S(2)}) copy-start(s32[128]{0:T(128)} %param.22) | copy-start | bytes 1540
  221.5 15.9 %copy-start.1 = (f32[128]{0:T(128)S(1)}, f32[128]{0:T(128)}, u32[]{:S(2)}) copy-start(f32[128]{0:T(128)} %param.23) | copy-start | bytes 1540
  236.2 3.8 %collective-permute-start = (bf16[128,6400]{1,0:T(8,128)(2,1)}, bf16[128,6400]{1,0:T(8,128)(2,1)}, u32[]{:S(2)}, u32[]{:S(2)}) collective-permute-start(bf16[128,6400]{1,0:T(8,128)(2,1)} %get-tuple-element.12), channel_id=1, source_target_pairs={{0,16},{16,0},{1,17},{17,1},{2,18},{18,2},{3,19},{19,3},{4,20},{20... | collective-permute-start | bytes 4915208 | tf_op jit(solution)/shard_map/ppermute | solution.py:12
Sparse Core Ops, SparseCore 0:
  110.6 109.4 all-reduce.1
where the time goes:
time: 258 us
  waiting for transfers between devices  111 us (43%)
  blocking collectives  83.9 us (33%)
  matrix products  29.5 us (11%)
  between operations  13.5 us (5%)
  local copies, waits for them, and re-layouts  10.7 us (4%)
  other arithmetic  9.26 us (4%)
    psum x1, waiting for transfers between devices, body(): summed = lax.psum(partial_sum, 'blk')  110 us
    all_gather x1, blocking collectives, body(): lax.all_gather(value_rows, 'blk', axis=0, tiled=True)  45.3 us
    all_gather x1, blocking collectives, body(): rows_full = lax.all_gather(residual, 'blk', axis=1, tiled=True)  38.5 us
    dot_general x1, matrix products, body(): jnp.dot(rms_round(after_mlp, head_gain), w_head, preferred_element_type=j...  14.7 us
  transfers between devices with their start and end apart: 2, of which 2 were waited for; matrix products, arithmetic and copies ran while one was open for 1% of the time, Pallas kernels for 0%

commit v1 on v0

--- a/solution.py
+++ b/solution.py
@@ -91,7 +91,7 @@
         unit_ids[None, :] < FF, jax.nn.silu(gate_out) * up_out, jnp.float32(0.0)
     ).astype(jnp.bfloat16)
     partial_sum = jnp.dot(hidden, w_down, preferred_element_type=jnp.float32)
-    summed = lax.psum(partial_sum, "blk")
+    summed = jnp.sum(lax.all_gather(partial_sum, "blk"), axis=0)
     after_mlp = (rows_full.astype(jnp.float32) + summed).astype(jnp.bfloat16)
     logits = jnp.dot(rms_round(after_mlp, head_gain), w_head, preferred_element_type=jnp.float32)
     request_count = logits.shape[0]

time: 258 us -> 343 us (1.33)
  waiting for transfers between devices: 111 us -> 190 us
  other arithmetic: 9.26 us -> 15.7 us
    all_gather x0 -> x1, waiting for transfers between devices: none -> 189 us  [body(): summed = jnp.sum(lax.all_gather(partial_sum, 'blk'), axis=0)]
    psum x1 -> x0, waiting for transfers between devices: 110 us -> none  [body(): summed = lax.psum(partial_sum, 'blk')]
    reduce_sum x0 -> x1, other arithmetic: none -> 7.49 us  [body(): summed = jnp.sum(lax.all_gather(partial_sum, 'blk'), axis=0)]
where the time goes in v1:
time: 343 us
  waiting for transfers between devices  190 us (55%)
  blocking collectives  83.9 us (24%)
  matrix products  28.6 us (8%)
  other arithmetic  15.7 us (5%)
  between operations  13.5 us (4%)
  local copies, waits for them, and re-layouts  10.7 us (3%)
    all_gather x1, waiting for transfers between devices, body(): summed = jnp.sum(lax.all_gather(partial_sum, 'blk'), axis=0)  189 us
    all_gather x1, blocking collectives, body(): lax.all_gather(value_rows, 'blk', axis=0, tiled=True)  45.3 us
    all_gather x1, blocking collectives, body(): rows_full = lax.all_gather(residual, 'blk', axis=1, tiled=True)  38.5 us
    dot_general x1, matrix products, body(): jnp.dot(rms_round(after_mlp, head_gain), w_head, preferred_element_type=j...  13.8 us
    reduce_sum x1, other arithmetic, body(): summed = jnp.sum(lax.all_gather(partial_sum, 'blk'), axis=0)  7.49 us
  transfers between devices with their start and end apart: 2, of which 2 were waited for; matrix products, arithmetic and copies ran while one was open for 1% of the time, Pallas kernels for 0%

profile of v1, /device:TPU:0, one launch (start us, length us, event | category | flops | bytes accessed | tf_op | source)
XLA Modules:
  0.0 343.0 jit_solution(13303615628374586665)
XLA Ops:
  6.5 0.0 copy-start
  6.5 0.0 all-gather.3.cloned.1.call-start
  6.6 1.4 gather_fusion.2
  8.0 1.3 gather_fusion.3
  9.4 0.1 iota_compare_fusion
  9.4 1.1 reshape.73
  10.5 0.7 slice_convert_fusion
  11.2 0.9 fusion.44
  12.1 2.2 fusion.55
  14.3 0.2 fusion.39
  14.5 0.1 copy.17
  14.6 0.0 copy-start.4
  14.6 0.0 copy-start.5
  14.6 0.0 copy-start.7
  14.6 2.4 fusion.4
  17.0 0.0 copy-done.4
  17.0 0.0 copy-start.8
  17.0 0.5 fusion.11
  17.5 45.3 %all_gather.12 = bf16[128,2048]{1,0:T(8,128)(2,1)S(1)} all-gather(bf16[8,2048]{1,0:T(8,128)(2,1)S(1)} %fusion.11), channel_id=1, replica_groups=mesh['guide'=2,'blk'=16] {'blk'}, dimensions={0}, use_global_device_ids=true | all-gather | bytes 557056 | tf_op jit(solution)/shard_map/all_gather | solution.py:79
  62.8 0.0 copy-done.5
  62.8 0.0 copy-done.7
  62.8 0.3 fusion.10
  63.1 38.5 %all_gather.13 = bf16[128,2048]{1,0:T(8,128)(2,1)S(1)} all-gather(bf16[128,128]{1,0:T(8,128)(2,1)S(1)} %fusion.10), channel_id=1, replica_groups=mesh['guide'=2,'blk'=16] {'blk'}, dimensions={1}, use_global_device_ids=true | all-gather | bytes 557056 | tf_op jit(solution)/shard_map/all_gather | solution.py:84
  101.7 0.2 fusion.15
  101.9 0.0 copy-done.8
  101.9 3.5 %fusion.34 = f32[128,684]{0,1:T(8,128)} fusion(bf16[2048,684]{0,1:T(8,128)(2,1)} %param.27, bf16[128,2048]{1,0:T(8,128)(2,1)S(1)} %all_gather.13, f32[2048]{0:T(1024)S(1)} %copy-done.8, f32[128]{0:T(128)S(1)} %add_rsqrt_fusion.1), kind=kOutput, calls=%fused_computation.49 | convolution fusion | flops 359661568 | bytes 3684864 | tf_op jit(solution)/shard_map/dot_general | solution.py:87
  105.4 0.0 copy-done
  105.4 5.0 %fusion.8 = f32[128,2048]{1,0:T(8,128)} fusion(bf16[684,2048]{1,0:T(8,128)(2,1)S(1)} %copy-done, bf16[2048,684]{0,1:T(8,128)(2,1)} %param.28, f32[128,684]{0,1:T(8,128)} %fusion.34, pred[684]{0:T(1024)(128)(4,1)S(1)} %add_compare_fusion, bf16[128,2048]{1,0:T(8,128)(2,1)S(1)} %all_gather.13, f32[2048]{0:T(1024)S(1)} %copy-done.8, f32[128]{0:T(128)S(1)} %add_rsqrt_fusion.1), kind=kOutput, calls=%fused_computation.21 | convolution fusion | flops 718887424 | bytes 7535788 | tf_op jit(solution)/shard_map/dot_general | solution.py:93
  110.4 0.0 all-gather.3.cloned.1.call-update
  110.5 189.4 %all-gather.3.cloned.1.call-done = f32[2048,2048]{1,0:T(8,128)} async-done(((f32[128,2048]{1,0:T(8,128)}), f32[2048,2048]{1,0:T(8,128)}) %all-gather.3.cloned.1.call-update) | async-done | bytes 16777232 | tf_op jit(solution)/shard_map/all_gather | solution.py:94
  299.8 0.0 copy-start.6
  299.8 7.5 %reduce_sum.38 = f32[128,2048]{1,0:T(8,128)S(1)} reduce(f32[16,128,2048]{2,1,0:T(8,128)} %bitcast.24, f32[]{:T(128)} %constant.46.clone.1), dimensions={0}, to_apply=%region_4.6 | reduce | flops 3932160 | bytes 17825796 | tf_op jit(solution)/shard_map/reduce_sum | solution.py:94
  307.3 0.2 fusion.12
  307.6 0.0 copy-done.6
  307.6 0.0 copy-start.3
  307.6 0.0 copy-start.2
  307.6 13.8 %fusion.56 = (bf16[128,6400]{1,0:T(8,128)(2,1)S(1)}, f32[128,6400]{1,0:T(8,128)}) fusion(bf16[2048,6400]{1,0:T(8,128)(2,1)} %param.31, f32[2048]{0:T(1024)S(1)} %copy-done.6, f32[128]{0:T(128)S(1)} %add_rsqrt_fusion, f32[128,2048]{1,0:T(8,128)S(1)} %reduce_sum.38, bf16[128,2048]{1,0:T(8,128)(2,1)S(1)} %all_gather.13), kind=kOutput, calls=%fused_computation.90 | convolution fusion | flops 3358097408 | bytes 32711168 | tf_op jit(solution)/shard_map/dot_general | solution.py:96
  321.4 0.0 collective-permute-start
  321.4 0.0 copy-done.3
  321.5 1.2 scatter_custom_fusion
  322.6 0.0 copy-done.2
  322.7 1.2 gather_fusion
  323.9 0.1 compare_and_fusion
  324.0 1.1 collective-permute-done
  325.1 4.5 %fusion.3 = bf16[128,6400]{1,0:T(8,128)(2,1)} fusion(f32[128,6400]{1,0:T(8,128)} %get-tuple-element.13, bf16[128,6400]{1,0:T(8,128)(2,1)} %collective-permute-done, f32[128]{0:T(128)S(1)} %and_select_fusion.2, pred[]{:T(512)S(6)} %eq.4), kind=kLoop, calls=%fused_computation.10 | loop fusion | flops 5734400 | bytes 6554113 | tf_op jit(solution)/shard_map/convert_element_type | solution.py:109
  329.6 4.3 %gather_fusion.1 = bf16[64,6400]{1,0:T(8,128)(2,1)} fusion(bf16[128,6400]{1,0:T(8,128)(2,1)} %fusion.3, s32[1024]{0:T(1024)S(1)} %pad_clamp_fusion), kind=kCustom, calls=%fused_computation.3 | custom fusion | bytes 1638656 | tf_op jit(solution)/shard_map/jit(_take)/gather | solution.py:112
  333.9 2.2 broadcast_select_fusion
  336.1 0.0 copy-done.1
  (16 shorter events, 0.1 us)
Async XLA Ops:
  6.5 98.9 %copy-start = (bf16[684,2048]{1,0:T(8,128)(2,1)S(1)}, bf16[684,2048]{1,0:T(8,128)(2,1)}, u32[]{:S(2)}) copy-start(bf16[684,2048]{1,0:T(8,128)(2,1)} %param.29) | copy-start | bytes 8404996
  6.5 293.3 %all-gather.3.cloned.1.call-start = ((), (), s32[]{:S(2)}) async-start(), calls=%async_computation | async-start | bytes 17825792 | tf_op jit(solution)/shard_map/all_gather | solution.py:94
  14.6 2.4 copy-start.4
  14.6 48.3 %copy-start.5 = (bf16[2048,128]{1,0:T(8,128)(2,1)S(1)}, bf16[2048,128]{1,0:T(8,128)(2,1)}, u32[]{:S(2)}) copy-start(bf16[2048,128]{1,0:T(8,128)(2,1)} %param.25) | copy-start | bytes 1572868
  14.6 48.3 %copy-start.7 = (bf16[128,128]{1,0:T(8,128)(2,1)S(1)}, bf16[128,128]{1,0:T(8,128)(2,1)}, u32[]{:S(2)}) copy-start(bf16[128,128]{1,0:T(8,128)(2,1)} %param.17) | copy-start | bytes 98308
  17.0 84.9 %copy-start.8 = (f32[2048]{0:T(1024)S(1)}, f32[2048]{0:T(1024)}, u32[]{:S(2)}) copy-start(f32[2048]{0:T(1024)} %param.26) | copy-start | bytes 24580
  299.8 7.7 %copy-start.6 = (f32[2048]{0:T(1024)S(1)}, f32[2048]{0:T(1024)}, u32[]{:S(2)}) copy-start(f32[2048]{0:T(1024)} %param.30) | copy-start | bytes 24580
  307.6 13.9 %copy-start.3 = (s32[128]{0:T(128)S(1)}, s32[128]{0:T(128)}, u32[]{:S(2)}) copy-start(s32[128]{0:T(128)} %param.22) | copy-start | bytes 1540
  307.6 15.1 %copy-start.2 = (f32[128]{0:T(128)S(1)}, f32[128]{0:T(128)}, u32[]{:S(2)}) copy-start(f32[128]{0:T(128)} %param.23) | copy-start | bytes 1540
  321.4 3.6 %collective-permute-start = (bf16[128,6400]{1,0:T(8,128)(2,1)S(1)}, bf16[128,6400]{1,0:T(8,128)(2,1)}, u32[]{:S(2)}, u32[]{:S(2)}) collective-permute-start(bf16[128,6400]{1,0:T(8,128)(2,1)S(1)} %get-tuple-element.12), channel_id=1, source_target_pairs={{0,16},{16,0},{1,17},{17,1},{2,18},{18,2},{3,19},{19,3},{4,20},{20... | collective-permute-start | bytes 4915208 | tf_op jit(solution)/shard_map/ppermute | solution.py:12
  325.1 11.0 %copy-start.1 = (bf16[684,2048]{1,0:T(8,128)(2,1)S(1)}, bf16[684,2048]{1,0:T(8,128)(2,1)}, u32[]{:S(2)}) copy-start(bf16[684,2048]{1,0:T(8,128)(2,1)} %param.29) | copy-start | bytes 8404996
Sparse Core Ops, SparseCore 0:
  110.6 189.2 all-gather.2
